TPU v7x, 512 devices: a whole 4x4x16 slice. The times are simulated.
512 devices in a mesh: dp: 64 (over y_lo, z, core), mp: 8 (over y_hi, x).
Axes of the slice: x: 4, y: 4 (y_hi: 2, y_lo: 2; y = y_hi * 2 + y_lo), z: 16, core: 2. Of those that a mesh axis runs over, the one named last changes fastest.
Arguments:
- acts: bfloat16 [16384, 28672], P('dp', 'mp'), may hold values from -24 to 24
- grads: bfloat16 [16384, 8192], P('dp', 'mp'), may hold values from -6 to 6
- basis_in: bfloat16 [28672, 640], P('mp', 'dp'), may hold values from -0.03125 to 0.03125
- basis_out: bfloat16 [8192, 1024], P('dp', 'mp'), may hold values from -0.0625 to 0.0625
- damping: float32 [1], replicated, may hold values from 0.5 to 2
Outputs:
- update: bfloat16 [28672, 8192], P('mp', 'dp')
- diag: float32 [640, 1024], P('mp', 'dp')
All inputs are finite; a program needn't handle non-finite values.
Results may differ from a plain program's by a relative error of at most 0.0085.
Values may be sent and summed in bfloat16 or wider, within the bound.
A program may use at most 64 MiB of HBM per device.

v0:
```python
import jax
import jax.numpy as jnp
from jax import lax
from jax.sharding import PartitionSpec as P


def on_device(acts, grads, basis_in, basis_out, damping):
    tok_rows = acts.shape[0]
    tokens_all = tok_rows * lax.axis_size("dp")
    whole_grads = lax.all_gather(grads, "mp", axis=1, tiled=True)
    grad_proj = jnp.dot(
        whole_grads,
        lax.all_gather(basis_out, "dp", axis=0, tiled=True),
        preferred_element_type=jnp.float32,
    ).astype(jnp.bfloat16)
    full_in = lax.all_gather(basis_in, "dp", axis=1, tiled=True)
    act_proj_t = lax.psum_scatter(
        lax.dot_general(
            full_in, acts, (((0,), (1,)), ((), ())), preferred_element_type=jnp.float32
        ),
        "mp",
        scatter_dimension=0,
        tiled=True,
    ).astype(jnp.bfloat16)
    act_sq_t = (act_proj_t.astype(jnp.float32) ** 2).astype(jnp.bfloat16)
    grad_sq = (grad_proj.astype(jnp.float32) ** 2).astype(jnp.bfloat16)
    stacked = jnp.stack([grad_proj, grad_sq])
    piece = lax.all_gather(stacked, "mp", axis=2, tiled=True)
    rotated = jnp.dot(act_proj_t, piece[0], preferred_element_type=jnp.float32)
    squares = jnp.dot(act_sq_t, piece[1], preferred_element_type=jnp.float32)
    partials = jnp.stack([rotated, squares])
    owned = lax.psum_scatter(partials, "dp", scatter_dimension=2, tiled=True)
    diag = owned[1] / tokens_all
    scaled = (owned[0] / (diag + damping[0])).astype(jnp.bfloat16)
    out_rows = lax.all_gather(basis_out, "mp", axis=1, tiled=True)
    dims = (((1,), (1,)), ((), ()))
    scaled_wide = lax.all_gather(scaled, "dp", axis=1, tiled=True)
    scaled_full = lax.all_gather(scaled_wide, "mp", axis=0, tiled=True)
    back = lax.dot_general(scaled_full, out_rows, dims, preferred_element_type=jnp.float32).astype(
        jnp.bfloat16
    )
    update = jnp.dot(full_in, back, preferred_element_type=jnp.float32)
    return (update.astype(jnp.bfloat16), diag)


def solution(mesh):
    placed = (P("dp", "mp"), P("dp", "mp"), P("mp", "dp"), P("dp", "mp"), P())
    return jax.shard_map(
        on_device,
        mesh=mesh,
        in_specs=placed,
        out_specs=(P("mp", "dp"), P("mp", "dp")),
        check_vma=False,
    )
```

profile of v0, /device:TPU:2, one launch (start us, length us, event | category | flops | bytes accessed | tf_op | source)
XLA Modules:
  0.0 1079.5 jit_solution(1085636390495247304)
XLA Ops:
  7.2 0.7 all-gather.9.cloned.1.call-update
  8.0 0.7 all-gather.7.cloned.1.call-update
  8.7 0.7 all-gather.15.cloned.1.call-update
  9.4 127.1 %all-gather.9.cloned.1.call-done = bf16[8192,128]{1,0:T(8,128)(2,1)} async-done(((bf16[128,128]{1,0:T(8,128)(2,1)}), bf16[8192,128]{1,0:T(8,128)(2,1)}) %all-gather.9.cloned.1.call-update) | async-done | bytes 2097168 | tf_op jit(solution)/shard_map/all_gather | solution.py:13
  136.6 85.5 %all-gather.7.cloned.1.call-done = bf16[256,8192]{1,0:T(8,128)(2,1)} async-done(((bf16[256,1024]{1,0:T(8,128)(2,1)}), bf16[256,8192]{1,0:T(8,128)(2,1)}) %all-gather.7.cloned.1.call-update) | async-done | bytes 4194320 | tf_op jit(solution)/shard_map/all_gather | solution.py:10
  222.1 4.1 convolution_convert_fusion.2
  226.2 0.7 pad_maximum_fusion.1
  227.0 123.7 %all-gather.15.cloned.1.call-done = bf16[64,10,3584]{2,1,0:T(8,128)(2,1)} async-done(((bf16[1,10,3584]{2,1,0:T(8,128)(2,1)}), bf16[64,10,3584]{2,1,0:T(8,128)(2,1)}) %all-gather.15.cloned.1.call-update) | async-done | bytes 4587536 | tf_op jit(solution)/shard_map/all_gather | solution.py:16
  350.6 8.0 reshape.7
  358.6 4.5 fusion.4
  363.2 50.1 %all-gather.11.cloned.1.call-done = bf16[2,256,1024]{2,1,0:T(8,128)(2,1)} async-done(((bf16[2,256,128]{2,1,0:T(8,128)(2,1)}), bf16[2,256,1024]{2,1,0:T(8,128)(2,1)}) %all-gather.11.cloned.1.call-update) | async-done | bytes 1048592 | tf_op jit(solution)/shard_map/all_gather | solution.py:28
  413.3 91.6 %reduce-scatter.2.cloned.1.call-done = f32[80,256]{1,0:T(8,128)} async-done(((f32[640,256]{1,0:T(8,128)}), f32[80,256]{1,0:T(8,128)}) %reduce-scatter.2.cloned.1.call-update) | async-done | bytes 81936 | tf_op jit(solution)/shard_map/reduce_scatter | solution.py:17
  504.9 1.3 convolution_bitcast_fusion
  506.2 1.3 convolution_bitcast_fusion.1
  507.5 1.3 copy.14
  509.6 1.3 dynamic-slice
  511.5 435.9 %all-reduce.3.cloned.1.call-done = f32[2,80,1024]{1,0,2:T(2,128)} async-done(((f32[2,80,1024]{1,0,2:T(2,128)}), f32[2,80,1024]{1,0,2:T(2,128)}) %all-reduce.3.cloned.1.call-update) | async-done | bytes 655376
  947.4 0.8 dynamic-slice_multiply_fusion
  948.2 62.7 %all_gather.25 = bf16[80,1024]{0,1:T(8,128)(2,1)S(1)} all-gather(bf16[80,16]{0,1:T(8,128)(2,1)S(1)} %divide_convert_fusion), channel_id=1, replica_groups=mesh['dp'=64,'mp'=8] {'dp'}, dimensions={1}, use_global_device_ids=true | all-gather | bytes 166400 | tf_op jit(solution)/shard_map/all_gather | solution.py:37
  1010.9 0.8 copy.16
  1011.7 30.1 %all_gather.27 = bf16[128,1024]{1,0:T(8,128)(2,1)S(1)} all-gather(bf16[128,128]{1,0:T(8,128)(2,1)S(1)} %copy-done.1), channel_id=1, replica_groups=mesh['dp'=64,'mp'=8] {'mp'}, dimensions={1}, use_global_device_ids=true | all-gather | bytes 294912 | tf_op jit(solution)/shard_map/all_gather | solution.py:35
  1041.8 24.9 %all-gather.13.cloned.1.call-done = bf16[640,1024]{1,0:T(8,128)(2,1)} async-done(((bf16[80,1024]{1,0:T(8,128)(2,1)}), bf16[640,1024]{1,0:T(8,128)(2,1)}) %all-gather.13.cloned.1.call-update) | async-done | bytes 1310736 | tf_op jit(solution)/shard_map/all_gather | solution.py:38
  1066.7 4.7 fusion
  1071.4 1.3 copy.17
  (20 shorter events, 0.4 us)
Async XLA Ops:
  7.2 351.5 %copy-start = (bf16[256,3584]{1,0:T(8,128)(2,1)S(1)}, bf16[256,3584]{1,0:T(8,128)(2,1)}, u32[]{:S(2)}) copy-start(bf16[256,3584]{1,0:T(8,128)(2,1)} %param.5) | copy-start | bytes 5505028
  7.2 129.4 %all-gather.9.cloned.1.call-start = ((), (), s32[]{:S(2)}) async-start(), calls=%async_computation.3 | async-start | bytes 2129920 | tf_op jit(solution)/shard_map/all_gather | solution.py:13
  7.9 214.2 %all-gather.7.cloned.1.call-start = ((), (), s32[]{:S(2)}) async-start(), calls=%async_computation.2 | async-start | bytes 4718592 | tf_op jit(solution)/shard_map/all_gather | solution.py:10
  8.7 342.0 %all-gather.15.cloned.1.call-start = ((), (), s32[]{:S(2)}) async-start(), calls=%async_computation.6 | async-start | bytes 7454720 | tf_op jit(solution)/shard_map/all_gather | solution.py:16
  9.4 403.9 %all-gather.11.cloned.1.call-start = ((), (), s32[]{:S(2)}) async-start(), calls=%async_computation.4 | async-start | bytes 1179648 | tf_op jit(solution)/shard_map/all_gather | solution.py:28
  226.9 277.9 %reduce-scatter.2.cloned.1.call-start = ((), (), s32[]{:S(2)}) async-start(), calls=%async_computation.1 | async-start | bytes 737280 | tf_op jit(solution)/shard_map/reduce_scatter | solution.py:17
  363.2 584.2 %all-reduce.3.cloned.1.call-start = ((), (), s32[]{:S(2)}) async-start(), calls=%async_computation.7 | async-start | bytes 2097152
  507.5 504.2 %copy-start.1 = (bf16[128,128]{1,0:T(8,128)(2,1)S(1)}, bf16[128,128]{1,0:T(8,128)(2,1)}, u32[]{:S(2)}) copy-start(bf16[128,128]{1,0:T(8,128)(2,1)} %param.8) | copy-start | bytes 98308
  508.9 557.8 %all-gather.13.cloned.1.call-start = ((), (), s32[]{:S(2)}) async-start(), calls=%async_computation.5 | async-start | bytes 1474560 | tf_op jit(solution)/shard_map/all_gather | solution.py:38
  948.2 123.2 %copy-start.2 = (f32[1,80,16]{1,0,2:T(1,128)}, f32[1,80,16]{1,0,2:T(1,128)S(1)}, u32[]{:S(2)}) copy-start(f32[1,80,16]{1,0,2:T(1,128)S(1)} %get-tuple-element.10) | copy-start | bytes 15364
Sparse Core Ops, SparseCore 0:
  10.1 126.3 all-gather.8
  139.8 82.2 all-gather.6
  224.3 126.3 all-gather.14
  353.5 59.7 all-gather.10
  418.2 86.6 reduce-scatter.1
  509.0 438.3 all-reduce.2
  1011.9 54.7 all-gather.12
where the time goes:
time: 1080 us
  waiting for transfers between devices  941 us (87%)
  blocking collectives  92.8 us (9%)
  matrix products  15.9 us (1%)
  between operations  15.5 us (1%)
  local copies, waits for them, and re-layouts  12.7 us (1%)
    unnamed x8, waiting for transfers between devices  438 us
    all_gather x1, waiting for transfers between devices, on_device(): lax.all_gather(basis_out, 'dp', axis=0, tiled=True)  127 us
    all_gather x1, waiting for transfers between devices, on_device(): full_in = lax.all_gather(basis_in, 'dp', axis=1, tiled=True)  124 us
    reduce_scatter x1, waiting for transfers between devices, on_device(): lax.psum_scatter(lax.dot_general(full_in, acts, (((0,), (1,)), ((), ())),...  91.6 us
    all_gather x1, waiting for transfers between devices, on_device(): whole_grads = lax.all_gather(grads, 'mp', axis=1, tiled=True)  85.5 us
    all_gather x1, blocking collectives, on_device(): scaled_wide = lax.all_gather(scaled, 'dp', axis=1, tiled=True)  62.7 us
    all_gather x1, waiting for transfers between devices, on_device(): piece = lax.all_gather(stacked, 'mp', axis=2, tiled=True)  50.1 us
    all_gather x1, blocking collectives, on_device(): out_rows = lax.all_gather(basis_out, 'mp', axis=1, tiled=True)  30.1 us
  transfers between devices with their start and end apart: 7, of which 7 were waited for; matrix products, arithmetic and copies ran while one was open for 2% of the time, Pallas kernels for 0%

commit v1 on v0

--- a/solution.py
+++ b/solution.py
@@ -10,7 +10,9 @@
     whole_grads = lax.all_gather(grads, "mp", axis=1, tiled=True)
     grad_proj = jnp.dot(
         whole_grads,
-        lax.all_gather(basis_out, "dp", axis=0, tiled=True),
+        jnp.concatenate(
+            lax.all_to_all(jnp.stack([basis_out] * lax.axis_size("dp")), "dp", 0, 0), axis=0
+        ),
         preferred_element_type=jnp.float32,
     ).astype(jnp.bfloat16)
     full_in = lax.all_gather(basis_in, "dp", axis=1, tiled=True)

time: 1080 us -> 967 us (0.90)
  waiting for transfers between devices: 941 us -> 808 us
  starting transfers between devices: 0.28 us -> 17.6 us
    all_gather x1 -> x0, waiting for transfers between devices: 127 us -> none  [on_device(): lax.all_gather(basis_out, 'dp', axis=0, tiled=True)]
    all_to_all x0 -> x1, starting transfers between devices: none -> 17.4 us  [on_device(): lax.all_to_all(jnp.stack([basis_out] * lax.axis_size('dp')), 'dp', 0, 0)]
    all_gather x1, waiting for transfers between devices: 124 us -> 108 us  [on_device(): full_in = lax.all_gather(basis_in, 'dp', axis=1, tiled=True)]
    all_to_all x0 -> x1, waiting for transfers between devices: none -> 14.5 us  [on_device(): lax.all_to_all(jnp.stack([basis_out] * lax.axis_size('dp')), 'dp', 0, 0)]
    unnamed x8 -> x7, waiting for transfers between devices: 438 us -> 437 us
where the time goes in v1:
time: 967 us
  waiting for transfers between devices  808 us (84%)
  blocking collectives  92.8 us (10%)
  starting transfers between devices  17.6 us (2%)
  matrix products  15.9 us (2%)
  between operations  15.5 us (2%)
  local copies, waits for them, and re-layouts  15.2 us (2%)
    unnamed x7, waiting for transfers between devices  437 us
    all_gather x1, waiting for transfers between devices, on_device(): full_in = lax.all_gather(basis_in, 'dp', axis=1, tiled=True)  108 us
    reduce_scatter x1, waiting for transfers between devices, on_device(): lax.psum_scatter(lax.dot_general(full_in, acts, (((0,), (1,)), ((), ())),...  91.6 us
    all_gather x1, waiting for transfers between devices, on_device(): whole_grads = lax.all_gather(grads, 'mp', axis=1, tiled=True)  81.8 us
    all_gather x1, blocking collectives, on_device(): scaled_wide = lax.all_gather(scaled, 'dp', axis=1, tiled=True)  62.7 us
    all_gather x1, waiting for transfers between devices, on_device(): piece = lax.all_gather(stacked, 'mp', axis=2, tiled=True)  50.1 us
    all_gather x1, blocking collectives, on_device(): out_rows = lax.all_gather(basis_out, 'mp', axis=1, tiled=True)  30.1 us
    all_gather x1, waiting for transfers between devices, on_device(): scaled_full = lax.all_gather(scaled_wide, 'mp', axis=0, tiled=True)  24.9 us
  transfers between devices with their start and end apart: 7, of which 7 were waited for; matrix products, arithmetic and copies ran while one was open for 2% of the time, Pallas kernels for 0%

profile of v1, /device:TPU:2, one launch (start us, length us, event | category | flops | bytes accessed | tf_op | source)
XLA Modules:
  0.0 966.7 jit_solution(13261859677522729579)
XLA Ops:
  7.2 0.7 all-gather.6.cloned.1.call-update
  8.0 0.7 all-gather.12.cloned.1.call-update
  8.7 2.6 stack.14
  11.2 17.4 %all-to-all-start = ((bf16[64,128,128]{2,1,0:T(8,128)(2,1)}), bf16[64,128,128]{2,1,0:T(8,128)(2,1)}, u32[]{:S(2)}, u32[]{:S(2)}) async-start(bf16[64,128,128]{2,1,0:T(8,128)(2,1)} %stack.14), calls=%async_computation.1 | async-start | bytes 4194304 | tf_op jit(solution)/shard_map/all_to_all | solution.py:14
  28.7 81.8 %all-gather.6.cloned.1.call-done = bf16[256,8192]{1,0:T(8,128)(2,1)} async-done(((bf16[256,1024]{1,0:T(8,128)(2,1)}), bf16[256,8192]{1,0:T(8,128)(2,1)}) %all-gather.6.cloned.1.call-update) | async-done | bytes 4194320 | tf_op jit(solution)/shard_map/all_gather | solution.py:10
  110.5 14.5 %all-to-all-done = bf16[64,128,128]{2,1,0:T(8,128)(2,1)} async-done(((bf16[64,128,128]{2,1,0:T(8,128)(2,1)}), bf16[64,128,128]{2,1,0:T(8,128)(2,1)}, u32[]{:S(2)}, u32[]{:S(2)}) %all-to-all-start) | async-done | bytes 2097184 | tf_op jit(solution)/shard_map/all_to_all | solution.py:14
  124.9 4.1 convolution_convert_fusion.2
  129.8 108.0 %all-gather.12.cloned.1.call-done = bf16[64,10,3584]{2,1,0:T(8,128)(2,1)} async-done(((bf16[1,10,3584]{2,1,0:T(8,128)(2,1)}), bf16[64,10,3584]{2,1,0:T(8,128)(2,1)}) %all-gather.12.cloned.1.call-update) | async-done | bytes 4587536 | tf_op jit(solution)/shard_map/all_gather | solution.py:18
  237.8 8.0 reshape.13
  245.8 4.5 fusion.4
  250.4 50.1 %all-gather.8.cloned.1.call-done = bf16[2,256,1024]{2,1,0:T(8,128)(2,1)} async-done(((bf16[2,256,128]{2,1,0:T(8,128)(2,1)}), bf16[2,256,1024]{2,1,0:T(8,128)(2,1)}) %all-gather.8.cloned.1.call-update) | async-done | bytes 1048592 | tf_op jit(solution)/shard_map/all_gather | solution.py:30
  300.5 91.6 %reduce-scatter.2.cloned.1.call-done = f32[80,256]{1,0:T(8,128)} async-done(((f32[640,256]{1,0:T(8,128)}), f32[80,256]{1,0:T(8,128)}) %reduce-scatter.2.cloned.1.call-update) | async-done | bytes 81936 | tf_op jit(solution)/shard_map/reduce_scatter | solution.py:19
  392.1 1.3 convolution_bitcast_fusion.1
  393.4 1.3 convolution_bitcast_fusion
  394.8 1.3 copy.14
  396.8 1.3 dynamic-slice
  398.7 435.8 %all-reduce.3.cloned.1.call-done = f32[2,80,1024]{1,0,2:T(2,128)} async-done(((f32[2,80,1024]{1,0,2:T(2,128)}), f32[2,80,1024]{1,0,2:T(2,128)}) %all-reduce.3.cloned.1.call-update) | async-done | bytes 655376
  834.6 0.8 dynamic-slice_multiply_fusion
  835.4 62.7 %all_gather.21 = bf16[80,1024]{0,1:T(8,128)(2,1)S(1)} all-gather(bf16[80,16]{0,1:T(8,128)(2,1)S(1)} %divide_convert_fusion), channel_id=1, replica_groups=mesh['dp'=64,'mp'=8] {'dp'}, dimensions={1}, use_global_device_ids=true | all-gather | bytes 166400 | tf_op jit(solution)/shard_map/all_gather | solution.py:39
  898.1 0.8 copy.16
  899.0 30.1 %all_gather.23 = bf16[128,1024]{1,0:T(8,128)(2,1)S(1)} all-gather(bf16[128,128]{1,0:T(8,128)(2,1)S(1)} %copy-done.1), channel_id=1, replica_groups=mesh['dp'=64,'mp'=8] {'mp'}, dimensions={1}, use_global_device_ids=true | all-gather | bytes 294912 | tf_op jit(solution)/shard_map/all_gather | solution.py:37
  929.0 24.9 %all-gather.10.cloned.1.call-done = bf16[640,1024]{1,0:T(8,128)(2,1)} async-done(((bf16[80,1024]{1,0:T(8,128)(2,1)}), bf16[640,1024]{1,0:T(8,128)(2,1)}) %all-gather.10.cloned.1.call-update) | async-done | bytes 1310736 | tf_op jit(solution)/shard_map/all_gather | solution.py:40
  953.9 4.7 fusion
  958.6 1.3 copy.17
  (20 shorter events, 1.1 us)
Async XLA Ops:
  7.2 238.6 %copy-start = (bf16[256,3584]{1,0:T(8,128)(2,1)S(1)}, bf16[256,3584]{1,0:T(8,128)(2,1)}, u32[]{:S(2)}) copy-start(bf16[256,3584]{1,0:T(8,128)(2,1)} %param.5) | copy-start | bytes 5505028
  7.2 103.3 %all-gather.6.cloned.1.call-start = ((), (), s32[]{:S(2)}) async-start(), calls=%async_computation.3 | async-start | bytes 4718592 | tf_op jit(solution)/shard_map/all_gather | solution.py:10
  7.9 229.9 %all-gather.12.cloned.1.call-start = ((), (), s32[]{:S(2)}) async-start(), calls=%async_computation.6 | async-start | bytes 7454720 | tf_op jit(solution)/shard_map/all_gather | solution.py:18
  11.2 113.7 %all-to-all-start = ((bf16[64,128,128]{2,1,0:T(8,128)(2,1)}), bf16[64,128,128]{2,1,0:T(8,128)(2,1)}, u32[]{:S(2)}, u32[]{:S(2)}) async-start(bf16[64,128,128]{2,1,0:T(8,128)(2,1)} %stack.14), calls=%async_computation.1 | async-start | bytes 4194304 | tf_op jit(solution)/shard_map/all_to_all | solution.py:14
  28.6 271.9 %all-gather.8.cloned.1.call-start = ((), (), s32[]{:S(2)}) async-start(), calls=%async_computation.4 | async-start | bytes 1179648 | tf_op jit(solution)/shard_map/all_gather | solution.py:30
  129.8 262.4 %reduce-scatter.2.cloned.1.call-start = ((), (), s32[]{:S(2)}) async-start(), calls=%async_computation.2 | async-start | bytes 737280 | tf_op jit(solution)/shard_map/reduce_scatter | solution.py:19
  250.3 584.3 %all-reduce.3.cloned.1.call-start = ((), (), s32[]{:S(2)}) async-start(), calls=%async_computation.7 | async-start | bytes 2097152
  394.8 504.2 %copy-start.1 = (bf16[128,128]{1,0:T(8,128)(2,1)S(1)}, bf16[128,128]{1,0:T(8,128)(2,1)}, u32[]{:S(2)}) copy-start(bf16[128,128]{1,0:T(8,128)(2,1)} %param.8) | copy-start | bytes 98308
  396.1 557.8 %all-gather.10.cloned.1.call-start = ((), (), s32[]{:S(2)}) async-start(), calls=%async_computation.5 | async-start | bytes 1474560 | tf_op jit(solution)/shard_map/all_gather | solution.py:40
  835.4 123.2 %copy-start.2 = (f32[1,80,16]{1,0,2:T(1,128)}, f32[1,80,16]{1,0,2:T(1,128)S(1)}, u32[]{:S(2)}) copy-start(f32[1,80,16]{1,0,2:T(1,128)S(1)} %get-tuple-element.10) | copy-start | bytes 15364
Sparse Core Ops, SparseCore 0:
  11.2 99.2 all-gather.5
  112.6 125.1 all-gather.11
  240.9 59.5 all-gather.7
  305.4 86.6 reduce-scatter.1
  396.2 438.2 all-reduce.2
  899.1 54.7 all-gather.9
